TPU v7x, 32 devices: a whole 2x2x4 slice. The times are simulated.
32 devices in a mesh: dp: 8 (over y, x, core), mp: 4 (over z).
Axes of the slice: x: 2, y: 2, z: 4, core: 2. Of those that a mesh axis runs over, the one named last changes fastest.
Arguments:
- features: bfloat16 [4, 4096, 1152], P('mp', 'dp'), may hold values from -6 to 6
- context_gain: float32 [1152], replicated, may hold values from 0.1 to 1.9
- queries: bfloat16 [64, 1536], replicated, may hold values from -136 to 136
- w_key: bfloat16 [1152, 384], replicated, may hold values from -0.1875 to 0.1875
- w_value: bfloat16 [1152, 384], replicated, may hold values from -0.1875 to 0.1875
- w_out: bfloat16 [1536, 2048], replicated, may hold values from -0.15625 to 0.15625
- image_tiles: int32 [4, 2], P('mp'), may hold values from 1024 to 3072, as said below
- slot_start: int32 [4, 2], P('mp'), may hold values from 0 to 64
- text_rows: bfloat16 [4, 1024, 2048], P('mp', 'dp'), may hold values from -6 to 6
- row_grads: bfloat16 [4, 1024, 2048], P('mp', 'dp'), may hold values from -6 to 6
Outputs:
- merged_rows: bfloat16 [4, 1024, 2048], P('mp', 'dp')
- query_grad: float32 [64, 1536], replicated
Inputs may be any that keep to these rules, and one draw needn't show every extreme that they name: `image_tiles`: the 2 images of a group fill its 4096 rows in order; every image takes 2 * 512 to 3072 rows, and in every group one image takes exactly 1024 and one exactly 3072.
All inputs are finite; a program needn't handle non-finite values.
Results may differ from a plain program's by a relative error of at most 0.005.
The roundings to bfloat16 on the way count: a program that leaves them out, or rounds other values in their place, can miss the bound.
Values may be sent and summed in bfloat16 or wider, within the bound.
A program may use at most 128 MiB of HBM per device.

v0:
```python
import jax
import jax.numpy as jnp
from jax import lax
from jax.sharding import PartitionSpec as P

HEADS = 16
HEAD = 96
KVH = 4
LAT = 64
DM = 2048
TOK_DEV = 512


epsilon = 1e-06


def prefix_2(value, axis, join, neutral, backward):
    count, mine = (lax.axis_size(axis), lax.axis_index(axis))
    pieces = jax.tree.map(lambda part: lax.all_gather(part, axis), value)
    if backward:
        pieces = jax.tree.map(lambda part: part[::-1], pieces)
        mine = count - 1 - mine
    so_far = jax.tree.map(
        lambda part, zero: jnp.full_like(part, 0) + jnp.asarray(zero, part.dtype), value, neutral
    )

    def lap(position, so_far):
        longer = join(so_far, jax.tree.map(lambda part: part[position], pieces))
        return jax.tree.map(lambda new, old: jnp.where(position < mine, new, old), longer, so_far)

    return lax.fori_loop(0, count - 1, lap, so_far)


def normalize(features, context_gain):
    widened = features.astype(jnp.float32)
    mean_square = jnp.mean(widened * widened, axis=-1, keepdims=True)
    return (widened * lax.rsqrt(mean_square + epsilon) * context_gain).astype(jnp.bfloat16)


def merge_partials(earlier, later):
    early_id, early_peak, early_total, early_sum = earlier
    late_id, late_peak, late_total, late_sum = later
    joint_peak = jnp.maximum(early_peak, late_peak)
    early_scale = jnp.exp(early_peak - joint_peak)
    late_scale = jnp.exp(late_peak - joint_peak)
    joined = (
        late_id,
        joint_peak,
        early_total * early_scale + late_total * late_scale,
        early_sum * early_scale[..., None] + late_sum * late_scale[..., None],
    )
    same_image = early_id == late_id
    keep_early = late_id < 0
    return jax.tree.map(
        lambda early_value, joint_value, late_value: jnp.where(
            keep_early, early_value, jnp.where(same_image, joint_value, late_value)
        ),
        earlier,
        joined,
        later,
    )


def take_nearest(earlier, later):
    return jax.tree.map(
        lambda early_value, late_value: jnp.where(later[0] >= 0, late_value, early_value),
        earlier,
        later,
    )


def partial_sums(scores, value_heads, mask):
    masked = jnp.where(mask, scores, -jnp.inf)
    row_peak = jnp.max(masked, axis=-1)
    row_peak = jnp.where(jnp.any(mask), row_peak, 0.0)
    weights = jnp.where(mask, jnp.exp(scores - row_peak[..., None]), 0.0)
    weight_total = jnp.sum(weights, axis=-1)
    summed = jnp.einsum(
        "gclr,rge->gcle",
        weights.astype(jnp.bfloat16),
        value_heads,
        preferred_element_type=jnp.float32,
    )
    return (row_peak, weight_total, summed)


def to_heads(rows):
    return rows.reshape(LAT, KVH, HEADS // KVH, HEAD).transpose(1, 2, 0, 3)


def on_device(
    features,
    context_gain,
    queries,
    w_key,
    w_value,
    w_out,
    image_tiles,
    slot_start,
    text_rows,
    row_grads,
):
    group_heads = HEADS // KVH
    scale = HEAD ** (-0.5)
    normed = normalize(features[0], context_gain)
    key_heads = (
        jnp.dot(normed, w_key, preferred_element_type=jnp.float32)
        .astype(jnp.bfloat16)
        .reshape(TOK_DEV, KVH, HEAD)
    )
    value_heads = (
        jnp.dot(normed, w_value, preferred_element_type=jnp.float32)
        .astype(jnp.bfloat16)
        .reshape(TOK_DEV, KVH, HEAD)
    )
    query_heads = queries.reshape(LAT, KVH, group_heads, HEAD)
    scores = (
        jnp.einsum("lgce,rge->gclr", query_heads, key_heads, preferred_element_type=jnp.float32)
        * scale
    )
    device = lax.axis_index("dp")
    first_row = device * TOK_DEV
    image_ends = jnp.cumsum(image_tiles[0])
    positions = first_row + jnp.arange(TOK_DEV, dtype=jnp.int32)
    image_of = jnp.sum((positions[:, None] >= image_ends[None, :]).astype(jnp.int32), axis=1)
    first_image = image_of[0]
    last_image = image_of[-1]
    in_first = image_of == first_image
    in_last = (image_of == last_image) & (last_image != first_image)
    first_part = partial_sums(scores, value_heads, in_first)
    last_part = partial_sums(scores, value_heads, in_last)
    same_image = first_image == last_image
    running_part = jax.tree.map(
        lambda first_value, last_value: jnp.where(same_image, first_value, last_value),
        first_part,
        last_part,
    )
    element = (last_image.astype(jnp.float32),) + running_part
    stat_shape = (KVH, group_heads, LAT)
    identity = (
        jnp.full((), -1.0, jnp.float32),
        jnp.zeros(stat_shape, jnp.float32),
        jnp.zeros(stat_shape, jnp.float32),
        jnp.zeros(stat_shape + (HEAD,), jnp.float32),
    )
    prefix = prefix_2(element, "dp", merge_partials, identity, False)
    finished = merge_partials(prefix, (first_image.astype(jnp.float32),) + first_part)
    ends_here = image_ends[first_image] <= first_row + TOK_DEV
    attended = finished[3] / finished[2][..., None]
    attended_rows = attended.transpose(2, 0, 1, 3).reshape(LAT, HEADS * HEAD)
    projected = jnp.dot(
        attended_rows.astype(jnp.bfloat16), w_out, preferred_element_type=jnp.float32
    ).astype(jnp.bfloat16)
    slot_row = slot_start[0][first_image]
    placed = lax.dynamic_update_slice(text_rows[0], projected, (slot_row, jnp.int32(0)))
    merged = jnp.where(ends_here, placed, text_rows[0])[None]
    taken_rows = lax.dynamic_slice(row_grads[0], (slot_row, jnp.int32(0)), (LAT, DM))
    grad_rows = jnp.einsum(
        "ld,ed->le", taken_rows, w_out, preferred_element_type=jnp.float32
    ).astype(jnp.bfloat16)
    inner_dot = jnp.sum(to_heads(grad_rows.astype(jnp.float32)) * attended, axis=-1)
    valid_id = jnp.where(ends_here, first_image, -1).astype(jnp.float32)
    own_payload = (finished[1], finished[2], inner_dot, grad_rows)
    ident_whole = (
        jnp.full((), -1.0, jnp.float32),
        jnp.zeros(stat_shape, jnp.float32),
        jnp.zeros(stat_shape, jnp.float32),
        jnp.zeros(stat_shape, jnp.float32),
        jnp.zeros((LAT, HEADS * HEAD), jnp.float32),
    )
    suffix = prefix_2(
        (valid_id, finished[1], finished[2], inner_dot, grad_rows.astype(jnp.float32)),
        "dp",
        take_nearest,
        ident_whole,
        True,
    )
    far_payload = (suffix[1], suffix[2], suffix[3], suffix[4].astype(jnp.bfloat16))
    near_payload = jax.tree.map(
        lambda own_value, far_value: jnp.where(ends_here, own_value, far_value),
        own_payload,
        far_payload,
    )
    row_first = in_first[None, None, None, :]
    peak_rows = jnp.where(row_first, near_payload[0][..., None], far_payload[0][..., None])
    total_rows = jnp.where(row_first, near_payload[1][..., None], far_payload[1][..., None])
    inner_rows = jnp.where(row_first, near_payload[2][..., None], far_payload[2][..., None])
    probability = jnp.exp(scores - peak_rows) / total_rows
    dot_first = jnp.einsum(
        "gcle,rge->gclr", to_heads(near_payload[3]), value_heads, preferred_element_type=jnp.float32
    )
    dot_last = jnp.einsum(
        "gcle,rge->gclr", to_heads(far_payload[3]), value_heads, preferred_element_type=jnp.float32
    )
    chosen = jnp.where(row_first, dot_first, dot_last)
    score_grad = (probability * (chosen - inner_rows)).astype(jnp.bfloat16)
    grad_term = jnp.einsum(
        "gclr,rge->lgce", score_grad, key_heads, preferred_element_type=jnp.float32
    )
    grad_term = grad_term.reshape(LAT, HEADS * HEAD) * scale
    query_grad = lax.psum(grad_term, ("dp", "mp"))
    return (merged, query_grad)


def solution(mesh):
    placed = (
        P("mp", "dp", None),
        P(),
        P(),
        P(),
        P(),
        P(),
        P("mp", None),
        P("mp", None),
        P("mp", "dp", None),
        P("mp", "dp", None),
    )
    return jax.shard_map(
        on_device, mesh=mesh, in_specs=placed, out_specs=(P("mp", "dp", None), P()), check_vma=False
    )
```

profile of v0, /device:TPU:0, one launch (start us, length us, event | category | flops | bytes accessed | tf_op | source)
XLA Modules:
  0.0 310.1 jit_solution(13000130615180911)
XLA Ops:
  7.2 2.0 copy.83
  9.2 0.8 reduce-window.4
  10.1 0.6 fusion.68
  12.8 1.2 constant_dynamic-slice_fusion
  16.0 5.7 %convolution_convert_fusion = bf16[64,1536]{1,0:T(8,128)(2,1)} fusion(bf16[1536,2048]{1,0:T(8,128)(2,1)} %param.19, bf16[1,128,2048]{2,1,0:T(8,128)(2,1)} %param.23, s32[]{:T(128)S(6)} %select_n.443), kind=kOutput, calls=%fused_computation.23 | convolution fusion | flops 402751488 | bytes 6750212 | tf_op jit(solution)/shard_map/ld,ed->le/dot_general | solution.py:158
  24.4 0.9 reshape.120
  25.7 2.1 fusion.67
  27.8 0.8 convolution_convert_fusion.3
  28.6 0.7 fusion.10
  29.3 2.1 broadcast_select_fusion.7
  31.4 0.8 convolution_convert_fusion.2
  32.3 0.6 fusion.26
  33.0 0.7 copy-done.3
  33.7 1.4 convolution_select_fusion
  35.2 0.7 constant_dynamic-slice_fusion.1
  37.9 0.6 dynamic-slice.6
  38.6 0.7 dynamic-update-slice.3
  39.3 0.7 dynamic-update-slice.2
  40.0 15.9 %all-reduce.2 = (f32[8]{0:T(128)}, f32[8]{0:T(128)S(1)}) all-reduce(f32[8]{0:T(128)S(1)} %dynamic-update-slice.2, f32[8]{0:T(128)S(1)} %dynamic-update-slice.3), channel_id=1, replica_groups=mesh['dp'=8,'mp'=4] {'dp'}, use_global_device_ids=true, to_apply=%add | all-reduce | flops 16 | bytes 128
  56.6 1.2 reshape.122
  57.9 0.6 rev.15
  58.5 3.0 fusion.20
  61.5 8.3 %all-gather.1 = f32[32,4,64]{2,1,0:T(4,128)S(1)} all-gather(f32[4,4,64]{2,1,0:T(4,128)S(1)} %bitcast.201), channel_id=3, replica_groups=mesh['dp'=8,'mp'=4] {'dp'}, dimensions={0}, use_global_device_ids=true | all-gather | bytes 36864 | tf_op jit(solution)/shard_map/all_gather | solution.py:19
  69.8 9.4 %all-gather = f32[32,4,64]{2,1,0:T(4,128)S(1)} all-gather(f32[4,4,64]{2,1,0:T(4,128)S(1)} %copy-done.16), channel_id=2, replica_groups=mesh['dp'=8,'mp'=4] {'dp'}, dimensions={0}, use_global_device_ids=true | all-gather | bytes 36864 | tf_op jit(solution)/shard_map/all_gather | solution.py:19
  79.2 1.5 rev.19
  80.7 8.4 %all-gather.10.cloned.1.call-done = f32[32,4,64,96]{3,2,1,0:T(8,128)} async-done(((f32[4,4,64,96]{3,2,1,0:T(8,128)}), f32[32,4,64,96]{3,2,1,0:T(8,128)}) %all-gather.10.cloned.1.call-update) | async-done | bytes 3145744 | tf_op jit(solution)/shard_map/all_gather | solution.py:19
  89.1 33.9 %while.40 = (s32[]{:T(128)}, f32[]{:T(128)}, f32[4,4,64]{2,1,0:T(4,128)S(1)}, f32[4,4,64]{2,1,0:T(4,128)S(1)}, f32[4,4,64,96]{3,2,1,0:T(8,128)S(1)}, /*index=5*/...) while((s32[]{:T(128)}, f32[]{:T(128)}, ...), condition=%wide.region_10.11_spmd.clone, body=%wide.region_9.10_spmd.clone.sunk | while | flops 702472 | bytes 1220823 | solution.py:31
  89.1 1.2 dynamic_slice.113
  91.7 1.6 select_select_fusion.14
  94.0 1.2 dynamic_slice.113
  96.5 1.6 select_select_fusion.14
  98.8 1.2 dynamic_slice.113
  101.4 1.6 select_select_fusion.14
  103.7 1.2 dynamic_slice.113
  106.2 1.6 select_select_fusion.14
  108.5 1.2 dynamic_slice.113
  111.1 1.6 select_select_fusion.14
  113.4 1.2 dynamic_slice.113
  115.9 1.6 select_select_fusion.14
  118.2 1.2 dynamic_slice.113
  120.8 1.6 select_select_fusion.14
  123.1 0.7 select_select_fusion.7
  123.8 9.1 %all-gather.4 = f32[32,4,64]{2,1,0:T(4,128)S(1)} all-gather(f32[4,4,64]{2,1,0:T(4,128)S(1)} %bitcast.191), channel_id=6, replica_groups=mesh['dp'=8,'mp'=4] {'dp'}, dimensions={0}, use_global_device_ids=true | all-gather | bytes 36864 | tf_op jit(solution)/shard_map/all_gather | solution.py:19
  132.9 2.4 fusion.42
  135.3 8.4 %all-gather.5 = f32[32,4,64]{2,1,0:T(4,128)S(1)} all-gather(f32[4,4,64]{2,1,0:T(4,128)S(1)} %get-tuple-element.502), channel_id=7, replica_groups=mesh['dp'=8,'mp'=4] {'dp'}, dimensions={0}, use_global_device_ids=true | all-gather | bytes 36864 | tf_op jit(solution)/shard_map/all_gather | solution.py:19
  143.7 9.3 %all-gather.3 = f32[32,4,64]{2,1,0:T(4,128)S(1)} all-gather(f32[4,4,64]{2,1,0:T(4,128)S(1)} %bitcast.197), channel_id=5, replica_groups=mesh['dp'=8,'mp'=4] {'dp'}, dimensions={0}, use_global_device_ids=true | all-gather | bytes 36864 | tf_op jit(solution)/shard_map/all_gather | solution.py:19
  153.0 10.0 %while.41 = (s32[]{:T(128)}, f32[4,4,64]{2,1,0:T(4,128)S(1)}, f32[4,4,64]{2,1,0:T(4,128)S(1)}, f32[4,4,64]{2,1,0:T(4,128)S(1)}, bf16[64,1536]{1,0:T(8,128)(2,1)S...) while((s32[]{:T(128)}, f32[4,4,64]{2,1,0:T(4,128)S(1)}, ...), condition=%wide.region_13.14_spmd.clone, body=%wide.region_12.13_spmd.clone.sunk | while | flops 304133 | bytes 626881 | solution.py:31
  153.0 0.6 dynamic_slice.117
  154.5 0.6 dynamic_slice.117
  155.9 0.6 dynamic_slice.117
  157.3 0.6 dynamic_slice.117
  158.7 0.6 dynamic_slice.117
  160.2 0.6 dynamic_slice.117
  161.6 0.6 dynamic_slice.117
  163.1 0.9 reshape.124
  164.0 0.9 reshape.123
  165.0 1.4 fusion.47
  166.4 3.9 %fusion.25 = f32[64,4,4,96]{3,0,2,1:T(8,128)} fusion(bf16[512,4,96,1]{0,2,3,1:T(8,128)(2,1)} %bitcast.208, f32[4,4,64,512]{3,2,1,0:T(8,128)S(1)} %fusion.47, f32[4,512,64,4]{1,2,3,0:T(8,128)} %copy-done.1, bf16[512,4,96,1]{0,2,3,1:T(8,128)(2,1)S(1)} %bitcast.180, f32[4,4,64]{2,1,0:T(4,128)S(1)} %get-tuple-element.368, f32[4,4,64]{2,1,0:T(4,128)S(1)} %bitcast.203, ...), kind=kOutput, calls=%fused_computation.52 | convolution fusion | flops 206143488 | bytes 5595648 | tf_op jit(solution)/shard_map/gclr,rge->lgce/dot_general | solution.py:197
  170.2 1.5 copy.28
  171.7 1.2 mul.145
  173.4 4.0 %fusion.8 = bf16[1,64,2048]{2,1,0:T(8,128)(2,1)S(1)} fusion(bf16[64,1536]{1,0:T(8,128)(2,1)S(1)} %convert_element_type.70, bf16[1536,2048]{1,0:T(8,128)(2,1)} %param.19, bf16[1,128,2048]{2,1,0:T(8,128)(2,1)S(1)} %copy-done.6, s32[]{:T(128)S(6)} %select_n.443, pred[]{:T(512)S(6)} %le.3), kind=kOutput, calls=%fused_computation.26 | convolution fusion | flops 402915328 | bytes 7012357 | tf_op jit(solution)/shard_map/dot_general | solution.py:151
  177.4 1.4 select_n.447
  178.8 123.0 %all-reduce.5.cloned.1.call-done = f32[64,1536]{1,0:T(8,128)} async-done(((f32[64,1536]{1,0:T(8,128)}), f32[64,1536]{1,0:T(8,128)}) %all-reduce.5.cloned.1.call-update) | async-done | bytes 393232 | tf_op jit(solution)/shard_map/psum | solution.py:201
  301.8 1.8 copy.85
  (104 shorter events, 2.7 us)
Async XLA Ops:
  7.2 20.6 %copy-start = (bf16[1152,384]{1,0:T(8,128)(2,1)S(1)}, bf16[1152,384]{1,0:T(8,128)(2,1)}, u32[]{:S(2)}) copy-start(bf16[1152,384]{1,0:T(8,128)(2,1)} %param.17) | copy-start | bytes 2654212
  7.2 72.0 %all-gather.12.cloned.1.call-start = ((), (), s32[]{:S(2)}) async-start(), calls=%async_computation.2 | async-start | bytes 1769472 | tf_op jit(solution)/shard_map/all_gather | solution.py:19
  16.0 8.4 %copy-start.12 = (bf16[64,1536]{1,0:T(8,128)(2,1)S(1)}, bf16[64,1536]{1,0:T(8,128)(2,1)}, u32[]{:S(2)}) copy-start(bf16[64,1536]{1,0:T(8,128)(2,1)} %param.16) | copy-start | bytes 589828
  16.0 9.4 %copy-start.8 = (bf16[1,512,1152]{2,1,0:T(8,128)(2,1)S(1)}, bf16[1,512,1152]{2,1,0:T(8,128)(2,1)}, u32[]{:S(2)}) copy-start(bf16[1,512,1152]{2,1,0:T(8,128)(2,1)} %param.14) | copy-start | bytes 3538948
  16.0 11.7 %copy-start.20 = (f32[1152]{0:T(1024)S(1)}, f32[1152]{0:T(1024)}, u32[]{:S(2)}) copy-start(f32[1152]{0:T(1024)} %param.15) | copy-start | bytes 13828
  21.7 67.4 %all-gather.10.cloned.1.call-start = ((), (), s32[]{:S(2)}) async-start(), calls=%async_computation.1 | async-start | bytes 4718592 | tf_op jit(solution)/shard_map/all_gather | solution.py:19
  25.7 3.0 copy-start.11
  27.7 30.7 %copy-start.17 = (pred[512]{0:T(512)(128)(4,1)}, pred[512]{0:T(512)(128)(4,1)S(1)}, u32[]{:S(2)}) copy-start(pred[512]{0:T(512)(128)(4,1)S(1)} %get-tuple-element.498) | copy-start | bytes 1540
  28.6 3.7 %copy-start.21 = (bf16[512,384]{0,1:T(8,128)(2,1)}, bf16[512,384]{0,1:T(8,128)(2,1)S(1)}, u32[]{:S(2)}) copy-start(bf16[512,384]{0,1:T(8,128)(2,1)S(1)} %convolution_convert_fusion.3) | copy-start | bytes 1179652
  28.6 2.8 copy-start.9
  28.6 2.8 copy-start.19
  29.3 3.6 %copy-start.1 = (f32[4,512,64,4]{1,2,3,0:T(8,128)}, f32[4,512,64,4]{1,2,3,0:T(8,128)S(1)}, u32[]{:S(2)}) copy-start(f32[4,512,64,4]{1,2,3,0:T(8,128)S(1)} %get-tuple-element.509) | copy-start | bytes 6291460
  31.4 27.1 %copy-start.13 = (f32[4,4,64]{2,1,0:T(4,128)}, f32[4,4,64]{2,1,0:T(4,128)S(1)}, u32[]{:S(2)}) copy-start(f32[4,4,64]{2,1,0:T(4,128)S(1)} %get-tuple-element.494) | copy-start | bytes 12292
  32.3 0.7 copy-start.4
  32.9 0.9 copy-start.3
  32.9 5.0 %copy-start.23 = (u32[32]{0:T(128)S(1)}, u32[32]{0:T(128)}, u32[]{:S(2)}) copy-start(u32[32]{0:T(128)} %constant.109) | copy-start | bytes 388
  32.9 23.7 %copy-start.2 = (bf16[64,1536]{1,0:T(8,128)(2,1)S(1)}, bf16[64,1536]{1,0:T(8,128)(2,1)}, u32[]{:S(2)}) copy-start(bf16[64,1536]{1,0:T(8,128)(2,1)} %convolution_convert_fusion) | copy-start | bytes 589828
  35.2 34.7 %copy-start.16 = (f32[4,4,64]{2,1,0:T(4,128)S(1)}, f32[4,4,64]{2,1,0:T(4,128)}, u32[]{:S(2)}) copy-start(f32[4,4,64]{2,1,0:T(4,128)} %get-tuple-element.492) | copy-start | bytes 12292
  35.2 266.6 %all-reduce.5.cloned.1.call-start = ((), (), s32[]{:S(2)}) async-start(), calls=%async_computation | async-start | bytes 786432 | tf_op jit(solution)/shard_map/psum | solution.py:201
  123.8 29.2 %copy-start.14 = (f32[2,8,64]{2,1,0:T(8,128)}, f32[2,8,64]{2,1,0:T(8,128)S(1)}, u32[]{:S(2)}) copy-start(f32[2,8,64]{2,1,0:T(8,128)S(1)} %get-tuple-element.536) | copy-start | bytes 12292
  123.8 29.2 %copy-start.22 = (f32[8]{0:T(128)S(1)}, f32[8]{0:T(128)}, u32[]{:S(2)}) copy-start(f32[8]{0:T(128)} %rev.15) | copy-start | bytes 100
  153.0 11.9 %copy-start.5 = (bf16[512,384]{0,1:T(8,128)(2,1)S(1)}, bf16[512,384]{0,1:T(8,128)(2,1)}, u32[]{:S(2)}) copy-start(bf16[512,384]{0,1:T(8,128)(2,1)} %copy-done.4) | copy-start | bytes 1179652
  163.0 3.3 %copy-start.15 = (f32[2,8,64]{2,1,0:T(8,128)S(1)}, f32[2,8,64]{2,1,0:T(8,128)}, u32[]{:S(2)}) copy-start(f32[2,8,64]{2,1,0:T(8,128)} %copy-done.14) | copy-start | bytes 12292
  163.0 3.3 %copy-start.18 = (pred[512]{0:T(512)(128)(4,1)S(1)}, pred[512]{0:T(512)(128)(4,1)}, u32[]{:S(2)}) copy-start(pred[512]{0:T(512)(128)(4,1)} %copy-done.17) | copy-start | bytes 1540
  170.2 2.7 copy-start.10
  170.2 3.2 %copy-start.6 = (bf16[1,128,2048]{2,1,0:T(8,128)(2,1)S(1)}, bf16[1,128,2048]{2,1,0:T(8,128)(2,1)}, u32[]{:S(2)}) copy-start(bf16[1,128,2048]{2,1,0:T(8,128)(2,1)} %copy.83) | copy-start | bytes 1572868
  178.8 124.8 %copy-start.7 = (bf16[1,128,2048]{2,1,0:T(8,128)(2,1)}, bf16[1,128,2048]{2,1,0:T(8,128)(2,1)S(1)}, u32[]{:S(2)}) copy-start(bf16[1,128,2048]{2,1,0:T(8,128)(2,1)S(1)} %select_n.447) | copy-start | bytes 1572868
Sparse Core Ops, SparseCore 0:
  21.9 28.3 all-gather.11
  52.2 36.9 all-gather.9
  173.0 128.6 all-reduce.4
where the time goes:
time: 311 us; the launch traced here: 310 us
  waiting for transfers between devices  131 us (42%)
  blocking collectives  60.4 us (19%)
  local copies, waits for them, and re-layouts  32.7 us (11%)
  other arithmetic  24.4 us (8%)
  between operations  23.5 us (8%)
  matrix products  19.2 us (6%)
  loops' own time  18.3 us (6%)
    psum x1, waiting for transfers between devices, on_device(): query_grad = lax.psum(grad_term, ('dp', 'mp'))  123 us
    all_gather x5, blocking collectives, prefix_2(): pieces = jax.tree.map(lambda part: lax.all_gather(part, axis), value)  44.5 us
    another operation x2, loops' own time, prefix_2(): return lax.fori_loop(0, count - 1, lap, so_far)  18.3 us
    unnamed x1, blocking collectives  15.9 us
    select_n x35, other arithmetic, lap(): jnp.where(position < mine, new, old)  12.8 us
    dynamic_slice x14, local copies, waits for them, and re-layouts, lap(): longer = join(so_far, jax.tree.map(lambda part: part[position], pieces))  12.8 us
    all_gather x2, waiting for transfers between devices, prefix_2(): pieces = jax.tree.map(lambda part: lax.all_gather(part, axis), value)  8.4 us
    unnamed x55, local copies, waits for them, and re-layouts  6.75 us
  transfers between devices with their start and end apart: 3, of which 2 were waited for; matrix products, arithmetic and copies ran while one was open for 8% of the time, Pallas kernels for 0%

commit v1 on v0

v1 whole, which is shorter than its diff:
```python
import functools

import jax
import jax.numpy as jnp
from jax import lax
from jax.experimental import pallas as pl
from jax.experimental.pallas import tpu as pltpu
from jax.sharding import PartitionSpec as P

HEADS = 16
HEAD = 96
KVH = 4
PER = HEADS // KVH
epsilon = 1e-06
LOW = -1e30
MESH = pl.DeviceIdType.MESH
F32 = jnp.float32
BF16 = jnp.bfloat16


def to_cols(rows):
    stacked = jnp.concatenate([rows[:, c * HEAD : (c + 1) * HEAD] for c in range(PER)], axis=0)
    return stacked.T


def to_rows(cols, lat):
    flipped = cols.T
    return jnp.concatenate(
        [
            flipped[c * lat : (c + 1) * lat, g * HEAD : (g + 1) * HEAD]
            for g in range(KVH)
            for c in range(PER)
        ],
        axis=1,
    )


def dot(a, b):
    return jnp.dot(a, b, preferred_element_type=F32)


class Gather:
    def __init__(self, chips, chip, core, at, send, recv):
        self.chips, self.chip, self.core = chips, chip, core
        self.at, self.send, self.recv = at, send, recv

    def hop(self, slot_chip, sem, target):
        ref = self.at(slot_chip, self.core)
        return pltpu.make_async_remote_copy(
            src_ref=ref,
            dst_ref=ref,
            send_sem=self.send.at[sem],
            recv_sem=self.recv.at[sem],
            device_id={"dp": target},
            device_id_type=MESH,
        )

    def start(self):
        for k in range(1, self.chips):
            there = lax.rem(self.chip + k, self.chips)
            self.hop(self.chip, k, there * 2 + self.core).start()
        self.hop(self.chip, 0, self.chip * 2 + 1 - self.core).start()

    def forward(self):
        for k in range(1, self.chips):
            origin = lax.rem(self.chip + self.chips - k, self.chips)
            self.hop(origin, k, origin * 2 + self.core).wait_recv()
            self.hop(origin, self.chips - 1 + k, self.chip * 2 + 1 - self.core).start()

    def finish(self):
        mate = self.chip * 2 + 1 - self.core
        for k in range(self.chips):
            origin = lax.rem(self.chip + self.chips - k, self.chips)
            ref = self.at(origin, 1 - self.core)
            sem = 0 if k == 0 else self.chips - 1 + k
            pltpu.make_async_remote_copy(
                src_ref=ref,
                dst_ref=ref,
                send_sem=self.send.at[sem],
                recv_sem=self.recv.at[sem],
                device_id={"dp": mate},
                device_id_type=MESH,
            ).wait_recv()
        for sem in range(2 * self.chips - 1):
            self.hop(self.chip, sem, mate).wait_send()


def kernel(
    dims,
    tiles,
    slots,
    gain,
    queries,
    features_hbm,
    wk_hbm,
    wv_hbm,
    wo_hbm,
    text_hbm,
    grads_hbm,
    merged,
    query_grad,
    features,
    wk,
    wv,
    wo,
    text,
    grads,
    keys,
    values,
    keys_t,
    values_t,
    query_t,
    weights,
    chosen,
    sums,
    u_own,
    u_recv,
    u_all,
    stats,
    g_own,
    g_recv,
    g_pair,
    g_chip,
    z_all,
    g_all,
    a_own,
    a_recv,
    a_pair,
    a_chip,
    a_all,
    load_sem,
    pair_send,
    pair_recv,
    u_send,
    u_got,
    s_send,
    s_got,
    gc_send,
    gc_got,
    z_send,
    z_got,
    g_send,
    g_got,
    ac_send,
    ac_got,
    a_send,
    a_got,
):
    n_dp, n_mp, images, lat, tok, seq = dims
    chips = n_dp // 2
    me = lax.axis_index("dp")
    z = lax.axis_index("mp")
    chip = lax.div(me, 2)
    core = lax.rem(me, 2)
    mate = chip * 2 + 1 - core
    scale = HEAD ** (-0.5)
    half = KVH * HEAD // 2
    block = KVH * HEAD

    loads = []

    def load(src, dst, at):
        copy = pltpu.make_async_copy(src, dst, load_sem.at[at])
        copy.start()
        return copy

    features_in = load(features_hbm, features, 0)
    grads_in = load(grads_hbm, grads, 1)
    wo_in = [
        load(wo_hbm.at[pl.ds(g * block, block)], wo.at[pl.ds(g * block, block)], 2 + g)
        for g in range(KVH)
    ]
    wk_in = load(wk_hbm, wk, 2 + KVH)
    wv_in = load(wv_hbm, wv, 3 + KVH)
    text_in = load(text_hbm, text, 4 + KVH)

    barrier = pltpu.get_barrier_semaphore()
    pl.semaphore_signal(barrier, inc=1, device_id={"dp": mate}, device_id_type=MESH)
    for k in range(1, chips):
        pl.semaphore_signal(
            barrier,
            inc=1,
            device_id={"dp": lax.rem(chip + k, chips) * 2 + core},
            device_id_type=MESH,
        )
    for k in range(1, n_mp):
        pl.semaphore_signal(
            barrier, inc=1, device_id={"mp": lax.rem(z + k, n_mp)}, device_id_type=MESH
        )

    def pair_copy(src, dst, at):
        return pltpu.make_async_remote_copy(
            src_ref=src,
            dst_ref=dst,
            send_sem=pair_send.at[at],
            recv_sem=pair_recv.at[at],
            device_id={"dp": mate},
            device_id_type=MESH,
        )

    first_row = me * tok
    ends = []
    running = jnp.int32(0)
    for i in range(images):
        running = running + tiles[0, i]
        ends.append(running)

    def image_at(row):
        found = jnp.int32(0)
        for end in ends:
            found = found + jnp.where(row >= end, 1, 0)
        return found

    def pick(options, index):
        chosen_one = options[0]
        for i in range(1, images):
            chosen_one = jnp.where(index == i, options[i], chosen_one)
        return chosen_one

    first = image_at(first_row)
    last = image_at(first_row + tok - 1)
    end_first = pick(ends, first)
    end_last = pick(ends, last)
    ends_here = end_first <= first_row + tok
    slot = pick([slots[0, i] for i in range(images)], first)
    slot = jnp.where(ends_here, slot, 2 * seq)
    rows_at = first_row + lax.broadcasted_iota(jnp.int32, (tok, 1), 0)
    in_first = rows_at < end_first

    features_in.wait()
    wide = features[0].astype(F32)
    mean_square = jnp.mean(wide * wide, axis=-1, keepdims=True)
    features[0] = (wide * lax.rsqrt(mean_square + epsilon) * gain[...]).astype(BF16)

    grads_in.wait()
    take = (
        lax.broadcasted_iota(jnp.int32, (lat, seq), 0) + slot
        == lax.broadcasted_iota(jnp.int32, (lat, seq), 1)
    )
    taken = dot(jnp.where(take, 1.0, 0.0).astype(BF16), grads[0]).astype(BF16)
    for g in range(KVH):
        wo_in[g].wait()
        up = lax.dot_general(
            taken,
            wo[g * block : (g + 1) * block, :],
            (((1,), (1,)), ((), ())),
            preferred_element_type=F32,
        )
        u_own[(g * HEAD) // half, pl.ds((g * HEAD) % half, HEAD), :] = to_cols(up).astype(BF16)
    pl.semaphore_wait(barrier, chips + n_mp - 1)
    u_pair = pair_copy(u_own.at[1 - core], u_recv, 0)
    u_pair.start()

    wk_in.wait()
    projected_keys = dot(features[0], wk[...])
    keys_t[...] = projected_keys.T.astype(BF16)
    for g in range(KVH):
        keys[g] = projected_keys[:, g * HEAD : (g + 1) * HEAD].astype(BF16)
    u_gather = Gather(chips, chip, core, lambda j, c: u_all.at[j, c], u_send, u_got)
    u_pair.wait()
    u_all[chip, core] = u_own[core] + u_recv[...]
    u_gather.start()
    wv_in.wait()
    projected_values = dot(features[0], wv[...])
    values_t[...] = projected_values.T.astype(BF16)
    for g in range(KVH):
        values[g] = projected_values[:, g * HEAD : (g + 1) * HEAD].astype(BF16)
    for g in range(KVH):
        query_t[g] = to_cols(queries[:, g * block : (g + 1) * block].astype(F32)).astype(BF16)

    peaks, totals = ([[], []], [[], []])
    for g in range(KVH):
        scores = dot(keys[g], query_t[g]) * scale
        peak_first = jnp.max(jnp.where(in_first, scores, LOW), axis=0, keepdims=True)
        peak_last = jnp.max(jnp.where(in_first, LOW, scores), axis=0, keepdims=True)
        weight = jnp.exp(scores - jnp.where(in_first, peak_first, peak_last))
        weights[g] = weight
        weight_first = jnp.where(in_first, weight, 0.0)
        weight_last = jnp.where(in_first, 0.0, weight)
        peaks[0].append(peak_first)
        peaks[1].append(peak_last)
        totals[0].append(jnp.sum(weight_first, axis=0, keepdims=True))
        totals[1].append(jnp.sum(weight_last, axis=0, keepdims=True))
        value_cols = values_t[pl.ds(g * HEAD, HEAD), :]
        sums[0, g] = dot(value_cols, weight_first.astype(BF16))
        sums[1, g] = dot(value_cols, weight_last.astype(BF16))
        if g == KVH - 2:
            u_gather.forward()
    u_gather.finish()

    chip_first = lax.div(end_first - 1, 2 * tok)
    chip_last = lax.div(end_last - 1, 2 * tok)

    def up_of(where_from, g):
        at = g * HEAD
        return u_all[where_from, at // half, pl.ds(at % half, HEAD), :]

    dots = [
        [
            jnp.sum(up_of(where_from, g).astype(F32) * sums[part, g], axis=0, keepdims=True)
            for g in range(KVH)
        ]
        for part, where_from in enumerate((chip_first, chip_last))
    ]
    stats[chip, core] = jnp.concatenate(
        peaks[0] + totals[0] + dots[0] + peaks[1] + totals[1] + dots[1], axis=0
    )
    s_gather = Gather(chips, chip, core, lambda j, c: stats.at[j, c], s_send, s_got)
    s_gather.start()
    for g in range(KVH):
        dot_first = dot(values[g], up_of(chip_first, g))
        dot_last = dot(values[g], up_of(chip_last, g))
        chosen[g] = jnp.where(in_first, dot_first, dot_last)
        if g == KVH // 2 - 1:
            s_gather.forward()
    s_gather.finish()

    own = stats[chip, core]
    parts = []
    for d in range(n_dp):
        got = stats[d // 2, d % 2]
        for part, image in enumerate((image_at(d * tok), image_at(d * tok + tok - 1))):
            at = 3 * KVH * part
            parts.append(
                (image, got[at : at + KVH], got[at + KVH : at + 2 * KVH], got[at + 2 * KVH : at + 3 * KVH])
            )

    def whole(mine, local_peak):
        peak = jnp.full_like(local_peak, LOW)
        for image, part_peak, _, _ in parts:
            peak = jnp.maximum(peak, jnp.where(image == mine, part_peak, LOW))
        total = jnp.zeros_like(peak)
        inner = jnp.zeros_like(peak)
        for image, part_peak, part_total, part_dot in parts:
            factor = jnp.where(image == mine, jnp.exp(part_peak - peak), 0.0)
            total = total + jnp.where(image == mine, part_total * factor, 0.0)
            inner = inner + jnp.where(image == mine, part_dot * factor, 0.0)
        return jnp.exp(local_peak - peak) / total, inner / total

    factor_first, inner_first = whole(first, own[0:KVH])
    factor_last, inner_last = whole(last, own[3 * KVH : 4 * KVH])

    for g in range(KVH):
        prob = weights[g] * jnp.where(
            in_first, factor_first[g : g + 1], factor_last[g : g + 1]
        )
        grad = prob * (
            chosen[g] - jnp.where(in_first, inner_first[g : g + 1], inner_last[g : g + 1])
        )
        term = dot(keys_t[pl.ds(g * HEAD, HEAD), :], grad.astype(BF16)) * scale
        lanes = term.shape[1] // 2
        for part in range(2):
            g_own[part, pl.ds(g * HEAD, HEAD), :] = term[:, part * lanes : (part + 1) * lanes]
    g_pair_copy = pair_copy(g_own.at[1 - core], g_recv, 1)
    g_pair_copy.start()

    for g in range(KVH):
        share_first = sums[0, g] * factor_first[g : g + 1]
        share_last = sums[1, g] * factor_last[g : g + 1]
        for i in range(images):
            share = jnp.where(first == i, share_first, 0.0) + jnp.where(last == i, share_last, 0.0)
            at = g * HEAD
            a_own[at // half, pl.ds(i * half + at % half, HEAD), :] = share.astype(BF16)
    a_pair_copy = pair_copy(a_own.at[1 - core], a_recv, 2)
    a_pair_copy.start()

    def scatter(src, rows, dst, send, recv, k, target_chip):
        return pltpu.make_async_remote_copy(
            src_ref=src.at[pl.ds(pl.multiple_of(target_chip * rows, rows), rows)],
            dst_ref=dst.at[k],
            send_sem=send.at[k],
            recv_sem=recv.at[k],
            device_id={"dp": target_chip * 2 + core},
            device_id_type=MESH,
        )

    g_rows = g_pair.shape[0] // chips
    a_rows = a_pair.shape[0] // chips
    g_pair_copy.wait()
    g_pair[...] = g_own[core] + g_recv[...]
    g_scatter = [
        scatter(g_pair, g_rows, g_chip, gc_send, gc_got, k, lax.rem(chip + k, chips))
        for k in range(1, chips)
    ]
    for copy in g_scatter:
        copy.start()
    a_pair_copy.wait()
    a_pair[...] = (a_own[core].astype(F32) + a_recv[...].astype(F32)).astype(BF16)
    a_scatter = [
        scatter(a_pair, a_rows, a_chip, ac_send, ac_got, k, lax.rem(chip + k, chips))
        for k in range(1, chips)
    ]
    for copy in a_scatter:
        copy.start()

    for copy in g_scatter:
        copy.wait()
    g_piece = g_pair[pl.ds(pl.multiple_of(chip * g_rows, g_rows), g_rows), :]
    for k in range(1, chips):
        g_piece = g_piece + g_chip[k]
    z_all[z] = g_piece
    z_copies = [
        pltpu.make_async_remote_copy(
            src_ref=z_all.at[z],
            dst_ref=z_all.at[z],
            send_sem=z_send.at[k],
            recv_sem=z_got.at[k],
            device_id={"mp": lax.rem(z + k, n_mp)},
            device_id_type=MESH,
        )
        for k in range(1, n_mp)
    ]
    for copy in z_copies:
        copy.start()

    for copy in a_scatter:
        copy.wait()
    a_piece = a_pair[pl.ds(pl.multiple_of(chip * a_rows, a_rows), a_rows), :].astype(F32)
    for k in range(1, chips):
        a_piece = a_piece + a_chip[k].astype(F32)
    a_all[core, pl.ds(pl.multiple_of(chip * a_rows, a_rows), a_rows), :] = a_piece.astype(BF16)
    a_gather = Gather(
        chips,
        chip,
        core,
        lambda j, c: a_all.at[c, pl.ds(pl.multiple_of(j * a_rows, a_rows), a_rows)],
        a_send,
        a_got,
    )
    a_gather.start()

    for k in range(1, n_mp):
        origin = lax.rem(z + n_mp - k, n_mp)
        pltpu.make_async_remote_copy(
            src_ref=z_all.at[origin],
            dst_ref=z_all.at[origin],
            send_sem=z_send.at[k],
            recv_sem=z_got.at[k],
            device_id={"mp": origin},
            device_id_type=MESH,
        ).wait_recv()
    g_sum = z_all[0]
    for k in range(1, n_mp):
        g_sum = g_sum + z_all[k]
    g_all[core, pl.ds(pl.multiple_of(chip * g_rows, g_rows), g_rows), :] = g_sum
    g_gather = Gather(
        chips,
        chip,
        core,
        lambda j, c: g_all.at[c, pl.ds(pl.multiple_of(j * g_rows, g_rows), g_rows)],
        g_send,
        g_got,
    )
    g_gather.start()
    for copy in z_copies:
        copy.wait_send()

    a_gather.forward()
    g_gather.forward()
    a_gather.finish()
    halves = []
    for part in range(2):
        attended = a_all[part, 0:half, :].astype(F32)
        for i in range(1, images):
            other = a_all[part, i * half : (i + 1) * half, :].astype(F32)
            attended = jnp.where(first == i, other, attended)
        halves.append(attended)
    attended_rows = to_rows(jnp.concatenate(halves, axis=0), lat).astype(BF16)
    put = (
        lax.broadcasted_iota(jnp.int32, (seq, lat), 1) + slot
        == lax.broadcasted_iota(jnp.int32, (seq, lat), 0)
    )
    shifted = dot(jnp.where(put, 1.0, 0.0).astype(BF16), attended_rows).astype(BF16)
    row_at = lax.broadcasted_iota(jnp.int32, (seq, 1), 0)
    inside = (row_at >= slot) & (row_at < slot + lat)
    text_in.wait()
    projected = dot(shifted, wo[...]).astype(BF16)
    merged[0] = jnp.where(inside, projected.astype(F32), text[0].astype(F32)).astype(BF16)

    g_gather.finish()
    query_grad[...] = to_rows(jnp.concatenate([g_all[0], g_all[1]], axis=1), lat)


def on_device(
    n_dp, n_mp, features, context_gain, queries, w_key, w_value, w_out, image_tiles, slot_start, text_rows, row_grads
):
    _, tok, width = features.shape
    images = image_tiles.shape[1]
    lat = queries.shape[0]
    _, seq, dm = text_rows.shape
    chips = n_dp // 2
    block = KVH * HEAD
    half = block // 2
    cols = PER * lat
    a_rows = images * half // chips
    g_rows = block // chips
    gathers = pltpu.SemaphoreType.DMA((2 * chips - 1,))
    vmem = pl.BlockSpec(memory_space=pltpu.VMEM)
    smem = pl.BlockSpec(memory_space=pltpu.SMEM)
    anywhere = pl.BlockSpec(memory_space=pl.ANY)
    return pl.pallas_call(
        functools.partial(kernel, (n_dp, n_mp, images, lat, tok, seq)),
        out_shape=(
            jax.ShapeDtypeStruct(text_rows.shape, BF16),
            jax.ShapeDtypeStruct(queries.shape, F32),
        ),
        in_specs=[smem, smem, vmem, vmem] + [anywhere] * 6,
        out_specs=(vmem, vmem),
        scratch_shapes=[
            pltpu.VMEM(features.shape, BF16),
            pltpu.VMEM(w_key.shape, BF16),
            pltpu.VMEM(w_value.shape, BF16),
            pltpu.VMEM(w_out.shape, BF16),
            pltpu.VMEM(text_rows.shape, BF16),
            pltpu.VMEM(row_grads.shape, BF16),
            pltpu.VMEM((KVH, tok, HEAD), BF16),
            pltpu.VMEM((KVH, tok, HEAD), BF16),
            pltpu.VMEM((block, tok), BF16),
            pltpu.VMEM((block, tok), BF16),
            pltpu.VMEM((KVH, HEAD, cols), BF16),
            pltpu.VMEM((KVH, tok, cols), F32),
            pltpu.VMEM((KVH, tok, cols), F32),
            pltpu.VMEM((2, KVH, HEAD, cols), F32),
            pltpu.VMEM((2, half, cols), BF16),
            pltpu.VMEM((half, cols), BF16),
            pltpu.VMEM((chips, 2, half, cols), BF16),
            pltpu.VMEM((chips, 2, 6 * KVH, cols), F32),
            pltpu.VMEM((2, block, cols // 2), F32),
            pltpu.VMEM((block, cols // 2), F32),
            pltpu.VMEM((block, cols // 2), F32),
            pltpu.VMEM((chips, g_rows, cols // 2), F32),
            pltpu.VMEM((n_mp, g_rows, cols // 2), F32),
            pltpu.VMEM((2, block, cols // 2), F32),
            pltpu.VMEM((2, images * half, cols), BF16),
            pltpu.VMEM((images * half, cols), BF16),
            pltpu.VMEM((images * half, cols), BF16),
            pltpu.VMEM((chips, a_rows, cols), BF16),
            pltpu.VMEM((2, images * half, cols), BF16),
            pltpu.SemaphoreType.DMA((5 + KVH,)),
            pltpu.SemaphoreType.DMA((3,)),
            pltpu.SemaphoreType.DMA((3,)),
            gathers,
            gathers,
            gathers,
            gathers,
            pltpu.SemaphoreType.DMA((chips,)),
            pltpu.SemaphoreType.DMA((chips,)),
            pltpu.SemaphoreType.DMA((n_mp,)),
            pltpu.SemaphoreType.DMA((n_mp,)),
            gathers,
            gathers,
            pltpu.SemaphoreType.DMA((chips,)),
            pltpu.SemaphoreType.DMA((chips,)),
            gathers,
            gathers,
        ],
        compiler_params=pltpu.CompilerParams(
            collective_id=0, has_side_effects=True, vmem_limit_bytes=60 * 1024 * 1024
        ),
        name="resampler",
    )(
        image_tiles,
        slot_start,
        context_gain.reshape(1, -1),
        queries,
        features,
        w_key,
        w_value,
        w_out,
        text_rows,
        row_grads,
    )


def solution(mesh):
    placed = (
        P("mp", "dp", None),
        P(),
        P(),
        P(),
        P(),
        P(),
        P("mp", None),
        P("mp", None),
        P("mp", "dp", None),
        P("mp", "dp", None),
    )
    return jax.shard_map(
        functools.partial(on_device, mesh.shape["dp"], mesh.shape["mp"]),
        mesh=mesh,
        in_specs=placed,
        out_specs=(P("mp", "dp", None), P()),
        check_vma=False,
    )
```

time: 311 us -> 47.7 us (0.15)
  waiting for transfers between devices: 131 us -> 0 us
  blocking collectives: 60.4 us -> 0 us
  Pallas kernels: 0 us -> 41.8 us
  local copies, waits for them, and re-layouts: 32.7 us -> 4.94 us
  other arithmetic: 24.4 us -> 0 us
  between operations: 23.5 us -> 0.64 us
  matrix products: 19.2 us -> 0 us
  loops' own time: 18.3 us -> 0 us
    psum x1 -> x0, waiting for transfers between devices: 123 us -> none  [on_device(): query_grad = lax.psum(grad_term, ('dp', 'mp'))]
    all_gather x5 -> x0, blocking collectives: 44.5 us -> none  [prefix_2(): pieces = jax.tree.map(lambda part: lax.all_gather(part, axis), value)]
    pallas_call x0 -> x1, Pallas kernels: none -> 41.8 us  [on_device(): pl.pallas_call(functools.partial(kernel, (n_dp, n_mp, images, lat, tok, s...]
    dot_general x9 -> x0, matrix products: 19.2 us -> none  [the longest x1 5.68 us: on_device(): jnp.einsum('ld,ed->le', taken_rows, w_out, preferred_element_type=jnp.flo...]
    another operation x2 -> x0, loops' own time: 18.3 us -> none  [prefix_2(): return lax.fori_loop(0, count - 1, lap, so_far)]
    unnamed x1 -> x0, blocking collectives: 15.9 us -> none
    select_n x41 -> x0, other arithmetic: 15.7 us -> none  [the longest x35 12.8 us: lap(): jnp.where(position < mine, new, old)]
    dynamic_slice x16 -> x0, local copies, waits for them, and re-layouts: 14.7 us -> none  [the longest x14 12.8 us: lap(): longer = join(so_far, jax.tree.map(lambda part: part[position], pieces))]
  transfers between devices with their start and end apart: 3 -> 0, of which waited for: 2 -> 0; matrix products, arithmetic and copies ran while one was open for 8% -> 0% of each run, Pallas kernels for 0% -> 0%
where the time goes in v1:
time: 47.7 us; the launch traced here: 47.4 us
  Pallas kernels  41.8 us (88%)
  local copies, waits for them, and re-layouts  4.94 us (10%)
  between operations  0.64 us (1%)
    pallas_call x1, Pallas kernels, on_device(): pl.pallas_call(functools.partial(kernel, (n_dp, n_mp, images, lat, tok, s...  41.8 us
    unnamed x2, local copies, waits for them, and re-layouts  3.65 us
    reshape x1, local copies, waits for them, and re-layouts, on_device(): context_gain.reshape(1, -1)  1.29 us

profile of v1, /device:TPU:0, one launch (start us, length us, event | category | flops | bytes accessed | tf_op | source)
XLA Modules:
  0.0 47.4 jit_solution(12740844500058396656)
XLA Ops:
  0.6 1.3 %reshape.7.gain = f32[1,1152]{1,0:T(1,128)} reshape(f32[1152]{0:T(1024)} %param.11) | data formatting | bytes 9216 | tf_op jit(solution)/shard_map/reshape | solution.py:564
  1.9 41.8 %resampler.1 = (bf16[1,128,2048]{2,1,0:T(8,128)(2,1)}, f32[64,1536]{1,0:T(8,128)}) custom-call(s32[1,2]{1,0:T(1,128)} %tiles.1, s32[1,2]{1,0:T(1,128)} %slots.1, f32[1,1152]{1,0:T(1,128)} %reshape.7.gain, bf16[64,1536]{1,0:T(8,128)(2,1)} %queries.1, bf16[1,512,1152]{2,1,0:T(8,128)(2,1)} %features_hbm.1, bf16[1152,384]{1,0:T(8,128)(2,1)} %wk_hbm.1, ...), custom_call_target="tpu_custom_call" | custom-call | tf_op jit(solution)/shard_map/resampler/pallas_call | solution.py:501
  43.8 1.9 %copy.14 = bf16[1,128,2048]{2,1,0:T(8,128)(2,1)} copy(bf16[1,128,2048]{2,1,0:T(8,128)(2,1)} %get-tuple-element.4) | data formatting | bytes 1048576
  45.7 1.8 %copy.15 = f32[64,1536]{1,0:T(8,128)} copy(f32[64,1536]{1,0:T(8,128)} %get-tuple-element.5) | data formatting | bytes 786432

commit v2 on v1

--- a/solution.py
+++ b/solution.py
@@ -83,6 +83,45 @@
             ).wait_recv()
         for sem in range(2 * self.chips - 1):
             self.hop(self.chip, sem, mate).wait_send()
+
+
+class Direct:
+    def __init__(self, chips, chip, core, src, dst, send, recv):
+        self.chips, self.chip, self.core = chips, chip, core
+        self.src, self.dst, self.send, self.recv = src, dst, send, recv
+
+    def hop(self, k, q, origin, target):
+        return pltpu.make_async_remote_copy(
+            src_ref=self.src(*target),
+            dst_ref=self.dst(*origin),
+            send_sem=self.send.at[2 * k + q],
+            recv_sem=self.recv.at[2 * k + q],
+            device_id={"dp": target[0] * 2 + target[1]},
+            device_id_type=MESH,
+        )
+
+    def other(self, k, q):
+        return (lax.rem(self.chip + k, self.chips), 1 - self.core if q else self.core)
+
+    def start(self, k, q):
+        self.hop(k, q, (self.chip, self.core), self.other(k, q)).start()
+
+    def all_start(self):
+        for k in list(range(1, self.chips)) + [0]:
+            for q in range(2):
+                if k or q:
+                    self.start(k, q)
+
+    def finish(self):
+        for k in range(self.chips):
+            for q in range(2):
+                if k or q:
+                    origin = self.other(self.chips - k, q)
+                    self.hop(k, q, origin, origin).wait_recv()
+        for k in range(self.chips):
+            for q in range(2):
+                if k or q:
+                    self.hop(k, q, (self.chip, self.core), self.other(k, q)).wait_send()
 
 
 def kernel(
@@ -117,9 +156,9 @@
     u_recv,
     u_all,
     stats,
+    dots,
+    rescale,
     g_own,
-    g_recv,
-    g_pair,
     g_chip,
     z_all,
     g_all,
@@ -135,6 +174,8 @@
     u_got,
     s_send,
     s_got,
+    d_send,
+    d_got,
     gc_send,
     gc_got,
     z_send,
@@ -164,24 +205,25 @@
         copy.start()
         return copy
 
+    def load_out(at, g):
+        part = pl.ds(pl.multiple_of(g * block, block), block)
+        return load(wo_hbm.at[part], wo.at[part], 2 + at)
+
+    half_groups = KVH // 2
+    order = [(1 - core) * half_groups + t for t in range(half_groups)]
+    order += [core * half_groups + t for t in range(half_groups)]
+    grads_in = load(grads_hbm, grads, 1)
+    wo_in = [load_out(t, order[t]) for t in range(half_groups)]
     features_in = load(features_hbm, features, 0)
-    grads_in = load(grads_hbm, grads, 1)
-    wo_in = [
-        load(wo_hbm.at[pl.ds(g * block, block)], wo.at[pl.ds(g * block, block)], 2 + g)
-        for g in range(KVH)
-    ]
+    wo_in += [load_out(t, order[t]) for t in range(half_groups, KVH)]
     wk_in = load(wk_hbm, wk, 2 + KVH)
     wv_in = load(wv_hbm, wv, 3 + KVH)
     text_in = load(text_hbm, text, 4 + KVH)
 
     barrier = pltpu.get_barrier_semaphore()
-    pl.semaphore_signal(barrier, inc=1, device_id={"dp": mate}, device_id_type=MESH)
-    for k in range(1, chips):
+    for k in range(1, n_dp):
         pl.semaphore_signal(
-            barrier,
-            inc=1,
-            device_id={"dp": lax.rem(chip + k, chips) * 2 + core},
-            device_id_type=MESH,
+            barrier, inc=1, device_id={"dp": lax.rem(me + k, n_dp)}, device_id_type=MESH
         )
     for k in range(1, n_mp):
         pl.semaphore_signal(
@@ -227,46 +269,54 @@
     rows_at = first_row + lax.broadcasted_iota(jnp.int32, (tok, 1), 0)
     in_first = rows_at < end_first
 
+    for g in range(KVH):
+        query_t[g] = to_cols(queries[:, g * block : (g + 1) * block].astype(F32)).astype(BF16)
+
+    grads_in.wait()
+    take = (
+        lax.broadcasted_iota(jnp.int32, (lat, seq), 0) + slot
+        == lax.broadcasted_iota(jnp.int32, (lat, seq), 1)
+    )
+    taken = dot(jnp.where(take, 1.0, 0.0).astype(BF16), grads[0]).astype(BF16)
+
+    def upstream(t):
+        wo_in[t].wait()
+        up = lax.dot_general(
+            taken,
+            wo[pl.ds(pl.multiple_of(order[t] * block, block), block), :],
+            (((1,), (1,)), ((), ())),
+            preferred_element_type=F32,
+        )
+        owner = 1 - core if t < half_groups else core
+        u_own[owner, pl.ds((t % half_groups) * HEAD, HEAD), :] = to_cols(up).astype(BF16)
+
+    for t in range(half_groups):
+        upstream(t)
+    pl.semaphore_wait(barrier, n_dp + n_mp - 2)
+    u_pair = pair_copy(u_own.at[1 - core], u_recv, 0)
+    u_pair.start()
+    for t in range(half_groups, KVH):
+        upstream(t)
+    u_gather = Gather(chips, chip, core, lambda j, c: u_all.at[j, c], u_send, u_got)
+    u_pair.wait()
+    u_all[chip, core] = u_own[core] + u_recv[...]
+    u_gather.start()
+
     features_in.wait()
     wide = features[0].astype(F32)
     mean_square = jnp.mean(wide * wide, axis=-1, keepdims=True)
     features[0] = (wide * lax.rsqrt(mean_square + epsilon) * gain[...]).astype(BF16)
-
-    grads_in.wait()
-    take = (
-        lax.broadcasted_iota(jnp.int32, (lat, seq), 0) + slot
-        == lax.broadcasted_iota(jnp.int32, (lat, seq), 1)
-    )
-    taken = dot(jnp.where(take, 1.0, 0.0).astype(BF16), grads[0]).astype(BF16)
-    for g in range(KVH):
-        wo_in[g].wait()
-        up = lax.dot_general(
-            taken,
-            wo[g * block : (g + 1) * block, :],
-            (((1,), (1,)), ((), ())),
-            preferred_element_type=F32,
-        )
-        u_own[(g * HEAD) // half, pl.ds((g * HEAD) % half, HEAD), :] = to_cols(up).astype(BF16)
-    pl.semaphore_wait(barrier, chips + n_mp - 1)
-    u_pair = pair_copy(u_own.at[1 - core], u_recv, 0)
-    u_pair.start()
 
     wk_in.wait()
     projected_keys = dot(features[0], wk[...])
     keys_t[...] = projected_keys.T.astype(BF16)
     for g in range(KVH):
         keys[g] = projected_keys[:, g * HEAD : (g + 1) * HEAD].astype(BF16)
-    u_gather = Gather(chips, chip, core, lambda j, c: u_all.at[j, c], u_send, u_got)
-    u_pair.wait()
-    u_all[chip, core] = u_own[core] + u_recv[...]
-    u_gather.start()
     wv_in.wait()
     projected_values = dot(features[0], wv[...])
     values_t[...] = projected_values.T.astype(BF16)
     for g in range(KVH):
         values[g] = projected_values[:, g * HEAD : (g + 1) * HEAD].astype(BF16)
-    for g in range(KVH):
-        query_t[g] = to_cols(queries[:, g * block : (g + 1) * block].astype(F32)).astype(BF16)
 
     peaks, totals = ([[], []], [[], []])
     for g in range(KVH):
@@ -284,35 +334,16 @@
         value_cols = values_t[pl.ds(g * HEAD, HEAD), :]
         sums[0, g] = dot(value_cols, weight_first.astype(BF16))
         sums[1, g] = dot(value_cols, weight_last.astype(BF16))
-        if g == KVH - 2:
-            u_gather.forward()
-    u_gather.finish()
-
-    chip_first = lax.div(end_first - 1, 2 * tok)
-    chip_last = lax.div(end_last - 1, 2 * tok)
-
-    def up_of(where_from, g):
-        at = g * HEAD
-        return u_all[where_from, at // half, pl.ds(at % half, HEAD), :]
-
-    dots = [
-        [
-            jnp.sum(up_of(where_from, g).astype(F32) * sums[part, g], axis=0, keepdims=True)
-            for g in range(KVH)
-        ]
-        for part, where_from in enumerate((chip_first, chip_last))
-    ]
-    stats[chip, core] = jnp.concatenate(
-        peaks[0] + totals[0] + dots[0] + peaks[1] + totals[1] + dots[1], axis=0
-    )
-    s_gather = Gather(chips, chip, core, lambda j, c: stats.at[j, c], s_send, s_got)
-    s_gather.start()
-    for g in range(KVH):
-        dot_first = dot(values[g], up_of(chip_first, g))
-        dot_last = dot(values[g], up_of(chip_last, g))
-        chosen[g] = jnp.where(in_first, dot_first, dot_last)
-        if g == KVH // 2 - 1:
-            s_gather.forward()
+
+    def to_all(ref, send, recv):
+        return Direct(
+            chips, chip, core, lambda j, c: ref.at[chip, core], lambda j, c: ref.at[j, c], send, recv
+        )
+
+    stats[chip, core] = jnp.concatenate(peaks[0] + totals[0] + peaks[1] + totals[1], axis=0)
+    s_gather = to_all(stats, s_send, s_got)
+    s_gather.all_start()
+    u_gather.forward()
     s_gather.finish()
 
     own = stats[chip, core]
@@ -320,43 +351,96 @@
     for d in range(n_dp):
         got = stats[d // 2, d % 2]
         for part, image in enumerate((image_at(d * tok), image_at(d * tok + tok - 1))):
-            at = 3 * KVH * part
-            parts.append(
-                (image, got[at : at + KVH], got[at + KVH : at + 2 * KVH], got[at + 2 * KVH : at + 3 * KVH])
-            )
+            at = 2 * KVH * part
+            parts.append((image, got[at : at + KVH], got[at + KVH : at + 2 * KVH]))
 
     def whole(mine, local_peak):
         peak = jnp.full_like(local_peak, LOW)
-        for image, part_peak, _, _ in parts:
+        for image, part_peak, _ in parts:
             peak = jnp.maximum(peak, jnp.where(image == mine, part_peak, LOW))
         total = jnp.zeros_like(peak)
-        inner = jnp.zeros_like(peak)
-        for image, part_peak, part_total, part_dot in parts:
-            factor = jnp.where(image == mine, jnp.exp(part_peak - peak), 0.0)
-            total = total + jnp.where(image == mine, part_total * factor, 0.0)
-            inner = inner + jnp.where(image == mine, part_dot * factor, 0.0)
-        return jnp.exp(local_peak - peak) / total, inner / total
-
-    factor_first, inner_first = whole(first, own[0:KVH])
-    factor_last, inner_last = whole(last, own[3 * KVH : 4 * KVH])
-
+        for image, part_peak, part_total in parts:
+            share = part_total * jnp.exp(part_peak - peak)
+            total = total + jnp.where(image == mine, share, 0.0)
+        return jnp.exp(local_peak - peak) / total
+
+    factors = (whole(first, own[0:KVH]), whole(last, own[2 * KVH : 3 * KVH]))
+    for part in range(2):
+        for g in range(KVH):
+            rescale[part, g] = factors[part][g : g + 1]
+            sums[part, g] = sums[part, g] * factors[part][g : g + 1]
+    u_gather.finish()
+
+    chip_first = lax.div(end_first - 1, 2 * tok)
+    chip_last = lax.div(end_last - 1, 2 * tok)
+
+    def up_of(where_from, g):
+        at = g * HEAD
+        return u_all[where_from, at // half, pl.ds(at % half, HEAD), :]
+
+    dots[chip, core] = jnp.concatenate(
+        [
+            jnp.sum(up_of(where_from, g).astype(F32) * sums[part, g], axis=0, keepdims=True)
+            for part, where_from in enumerate((chip_first, chip_last))
+            for g in range(KVH)
+        ],
+        axis=0,
+    )
+    d_gather = to_all(dots, d_send, d_got)
+    d_gather.all_start()
     for g in range(KVH):
-        prob = weights[g] * jnp.where(
-            in_first, factor_first[g : g + 1], factor_last[g : g + 1]
-        )
-        grad = prob * (
-            chosen[g] - jnp.where(in_first, inner_first[g : g + 1], inner_last[g : g + 1])
-        )
-        term = dot(keys_t[pl.ds(g * HEAD, HEAD), :], grad.astype(BF16)) * scale
+        dot_first = dot(values[g], up_of(chip_first, g))
+        dot_last = dot(values[g], up_of(chip_last, g))
+        chosen[g] = jnp.where(in_first, dot_first, dot_last)
+        weights[g] = weights[g] * jnp.where(in_first, rescale[0, g], rescale[1, g])
+    d_gather.finish()
+
+    inner_first = jnp.zeros((KVH, dots.shape[3]), F32)
+    inner_last = inner_first
+    for d in range(n_dp):
+        got = dots[d // 2, d % 2]
+        for part, image in enumerate((image_at(d * tok), image_at(d * tok + tok - 1))):
+            piece = got[part * KVH : (part + 1) * KVH]
+            inner_first = inner_first + jnp.where(image == first, piece, 0.0)
+            inner_last = inner_last + jnp.where(image == last, piece, 0.0)
+    for g in range(KVH):
+        rescale[0, g] = inner_first[g : g + 1]
+        rescale[1, g] = inner_last[g : g + 1]
+
+    g_rows = g_own.shape[2]
+    per_group = chips // KVH
+    g_scatter = Direct(
+        chips,
+        chip,
+        core,
+        lambda j, c: g_own.at[c, j],
+        lambda j, c: g_chip.at[j, c],
+        gc_send,
+        gc_got,
+    )
+    my_group = lax.div(chip, per_group)
+    for t in (1, 3, 2, 0):
+        g = lax.rem(my_group + t, KVH)
+        inner = jnp.where(in_first, rescale[0, g], rescale[1, g])
+        grad = weights[g] * (chosen[g] - inner)
+        cols_t = keys_t[pl.ds(pl.multiple_of(g * HEAD, HEAD), HEAD), :]
+        term = (dot(cols_t, grad.astype(BF16)) * scale)
         lanes = term.shape[1] // 2
-        for part in range(2):
-            g_own[part, pl.ds(g * HEAD, HEAD), :] = term[:, part * lanes : (part + 1) * lanes]
-    g_pair_copy = pair_copy(g_own.at[1 - core], g_recv, 1)
-    g_pair_copy.start()
+        for p in range(per_group):
+            for c in range(2):
+                g_own[c, g * per_group + p] = term[
+                    p * g_rows : (p + 1) * g_rows, c * lanes : (c + 1) * lanes
+                ].astype(BF16)
+        if per_group == 1:
+            for q in range(2):
+                if t or q:
+                    g_scatter.start(t, q)
+    if per_group != 1:
+        g_scatter.all_start()
 
     for g in range(KVH):
-        share_first = sums[0, g] * factor_first[g : g + 1]
-        share_last = sums[1, g] * factor_last[g : g + 1]
+        share_first = sums[0, g]
+        share_last = sums[1, g]
         for i in range(images):
             share = jnp.where(first == i, share_first, 0.0) + jnp.where(last == i, share_last, 0.0)
             at = g * HEAD
@@ -374,16 +458,7 @@
             device_id_type=MESH,
         )
 
-    g_rows = g_pair.shape[0] // chips
     a_rows = a_pair.shape[0] // chips
-    g_pair_copy.wait()
-    g_pair[...] = g_own[core] + g_recv[...]
-    g_scatter = [
-        scatter(g_pair, g_rows, g_chip, gc_send, gc_got, k, lax.rem(chip + k, chips))
-        for k in range(1, chips)
-    ]
-    for copy in g_scatter:
-        copy.start()
     a_pair_copy.wait()
     a_pair[...] = (a_own[core].astype(F32) + a_recv[...].astype(F32)).astype(BF16)
     a_scatter = [
@@ -393,11 +468,11 @@
     for copy in a_scatter:
         copy.start()
 
-    for copy in g_scatter:
-        copy.wait()
-    g_piece = g_pair[pl.ds(pl.multiple_of(chip * g_rows, g_rows), g_rows), :]
-    for k in range(1, chips):
-        g_piece = g_piece + g_chip[k]
+    g_chip[chip, core] = g_own[core, chip]
+    g_scatter.finish()
+    g_piece = g_chip[0, 0].astype(F32)
+    for d in range(1, n_dp):
+        g_piece = g_piece + g_chip[d // 2, d % 2].astype(F32)
     z_all[z] = g_piece
     z_copies = [
         pltpu.make_async_remote_copy(
@@ -442,21 +517,13 @@
     g_sum = z_all[0]
     for k in range(1, n_mp):
         g_sum = g_sum + z_all[k]
-    g_all[core, pl.ds(pl.multiple_of(chip * g_rows, g_rows), g_rows), :] = g_sum
-    g_gather = Gather(
-        chips,
-        chip,
-        core,
-        lambda j, c: g_all.at[c, pl.ds(pl.multiple_of(j * g_rows, g_rows), g_rows)],
-        g_send,
-        g_got,
-    )
-    g_gather.start()
+    g_all[chip, core] = g_sum.astype(BF16)
+    g_gather = to_all(g_all, g_send, g_got)
+    g_gather.all_start()
     for copy in z_copies:
         copy.wait_send()
 
     a_gather.forward()
-    g_gather.forward()
     a_gather.finish()
     halves = []
     for part in range(2):
@@ -478,7 +545,11 @@
     merged[0] = jnp.where(inside, projected.astype(F32), text[0].astype(F32)).astype(BF16)
 
     g_gather.finish()
-    query_grad[...] = to_rows(jnp.concatenate([g_all[0], g_all[1]], axis=1), lat)
+    whole_rows = [
+        jnp.concatenate([g_all[j, 0].astype(F32), g_all[j, 1].astype(F32)], axis=1)
+        for j in range(chips)
+    ]
+    query_grad[...] = to_rows(jnp.concatenate(whole_rows, axis=0), lat)
 
 
 def on_device(
@@ -495,14 +566,15 @@
     a_rows = images * half // chips
     g_rows = block // chips
     gathers = pltpu.SemaphoreType.DMA((2 * chips - 1,))
+    direct = pltpu.SemaphoreType.DMA((n_dp,))
     vmem = pl.BlockSpec(memory_space=pltpu.VMEM)
     smem = pl.BlockSpec(memory_space=pltpu.SMEM)
     anywhere = pl.BlockSpec(memory_space=pl.ANY)
     return pl.pallas_call(
         functools.partial(kernel, (n_dp, n_mp, images, lat, tok, seq)),
         out_shape=(
-            jax.ShapeDtypeStruct(text_rows.shape, BF16),
-            jax.ShapeDtypeStruct(queries.shape, F32),
+            pltpu.VMEM(text_rows.shape, BF16),
+            pltpu.VMEM(queries.shape, F32),
         ),
         in_specs=[smem, smem, vmem, vmem] + [anywhere] * 6,
         out_specs=(vmem, vmem),
@@ -524,13 +596,13 @@
             pltpu.VMEM((2, half, cols), BF16),
             pltpu.VMEM((half, cols), BF16),
             pltpu.VMEM((chips, 2, half, cols), BF16),
-            pltpu.VMEM((chips, 2, 6 * KVH, cols), F32),
-            pltpu.VMEM((2, block, cols // 2), F32),
-            pltpu.VMEM((block, cols // 2), F32),
-            pltpu.VMEM((block, cols // 2), F32),
-            pltpu.VMEM((chips, g_rows, cols // 2), F32),
+            pltpu.VMEM((chips, 2, 4 * KVH, cols), F32),
+            pltpu.VMEM((chips, 2, 2 * KVH, cols), F32),
+            pltpu.VMEM((2, KVH, 1, cols), F32),
+            pltpu.VMEM((2, chips, g_rows, cols // 2), BF16),
+            pltpu.VMEM((chips, 2, g_rows, cols // 2), BF16),
             pltpu.VMEM((n_mp, g_rows, cols // 2), F32),
-            pltpu.VMEM((2, block, cols // 2), F32),
+            pltpu.VMEM((chips, 2, g_rows, cols // 2), BF16),
             pltpu.VMEM((2, images * half, cols), BF16),
             pltpu.VMEM((images * half, cols), BF16),
             pltpu.VMEM((images * half, cols), BF16),
@@ -541,14 +613,16 @@
             pltpu.SemaphoreType.DMA((3,)),
             gathers,
             gathers,
-            gathers,
-            gathers,
-            pltpu.SemaphoreType.DMA((chips,)),
-            pltpu.SemaphoreType.DMA((chips,)),
+            direct,
+            direct,
+            direct,
+            direct,
+            direct,
+            direct,
             pltpu.SemaphoreType.DMA((n_mp,)),
             pltpu.SemaphoreType.DMA((n_mp,)),
-            gathers,
-            gathers,
+            direct,
+            direct,
             pltpu.SemaphoreType.DMA((chips,)),
             pltpu.SemaphoreType.DMA((chips,)),
             gathers,
@@ -561,7 +635,7 @@
     )(
         image_tiles,
         slot_start,
-        context_gain.reshape(1, -1),
+        context_gain,
         queries,
         features,
         w_key,

time: 47.7 us -> 38.2 us (0.80)
  Pallas kernels: 41.8 us -> 35.8 us
  local copies, waits for them, and re-layouts: 4.94 us -> 1.54 us
    pallas_call x1, Pallas kernels: 41.8 us -> 35.8 us  [on_device(): pl.pallas_call(functools.partial(kernel, (n_dp, n_mp, images, lat, tok, s...]
    unnamed x2, local copies, waits for them, and re-layouts: 3.65 us -> 1.54 us
    reshape x1 -> x0, local copies, waits for them, and re-layouts: 1.29 us -> none  [on_device(): context_gain.reshape(1, -1)]
where the time goes in v2:
time: 38.2 us; the launch traced here: 38 us
  Pallas kernels  35.8 us (94%)
  local copies, waits for them, and re-layouts  1.54 us (4%)
  between operations  0.64 us (2%)
    pallas_call x1, Pallas kernels, on_device(): pl.pallas_call(functools.partial(kernel, (n_dp, n_mp, images, lat, tok, s...  35.8 us
    unnamed x2, local copies, waits for them, and re-layouts  1.54 us

profile of v2, /device:TPU:0, one launch (start us, length us, event | category | flops | bytes accessed | tf_op | source)
XLA Modules:
  0.0 38.0 jit_solution(3219167862508395782)
XLA Ops:
  0.6 35.8 %resampler.1 = (bf16[1,128,2048]{2,1,0:T(8,128)(2,1)S(1)}, f32[64,1536]{1,0:T(8,128)S(1)}) custom-call(s32[1,2]{1,0:T(1,128)} %tiles.1, s32[1,2]{1,0:T(1,128)} %slots.1, f32[1152]{0:T(1024)} %gain.1, bf16[64,1536]{1,0:T(8,128)(2,1)} %queries.1, bf16[1,512,1152]{2,1,0:T(8,128)(2,1)} %features_hbm.1, bf16[1152,384]{1,0:T(8,128)(2,1)} %wk_hbm.1, ...), custom_call_target="tpu_custom_call" | custom-call | tf_op jit(solution)/shard_map/resampler/pallas_call | solution.py:573
  36.5 0.8 %copy.14 = bf16[1,128,2048]{2,1,0:T(8,128)(2,1)} copy(bf16[1,128,2048]{2,1,0:T(8,128)(2,1)S(1)} %get-tuple-element.2) | data formatting | bytes 1048576
  37.3 0.7 %copy.15 = f32[64,1536]{1,0:T(8,128)} copy(f32[64,1536]{1,0:T(8,128)S(1)} %get-tuple-element.3) | data formatting | bytes 786432

commit v3 on v2

--- a/solution.py
+++ b/solution.py
@@ -152,8 +152,8 @@
     weights,
     chosen,
     sums,
-    u_own,
-    u_recv,
+    t_own,
+    t_recv,
     u_all,
     stats,
     dots,
@@ -210,15 +210,15 @@
         return load(wo_hbm.at[part], wo.at[part], 2 + at)
 
     half_groups = KVH // 2
-    order = [(1 - core) * half_groups + t for t in range(half_groups)]
-    order += [core * half_groups + t for t in range(half_groups)]
+    order = [core * half_groups + t for t in range(half_groups)]
+    order += [(1 - core) * half_groups + t for t in range(half_groups)]
     grads_in = load(grads_hbm, grads, 1)
+    features_in = load(features_hbm, features, 0)
+    wk_in = load(wk_hbm, wk, 2 + KVH)
     wo_in = [load_out(t, order[t]) for t in range(half_groups)]
-    features_in = load(features_hbm, features, 0)
-    wo_in += [load_out(t, order[t]) for t in range(half_groups, KVH)]
-    wk_in = load(wk_hbm, wk, 2 + KVH)
     wv_in = load(wv_hbm, wv, 3 + KVH)
     text_in = load(text_hbm, text, 4 + KVH)
+    wo_in += [load_out(t, order[t]) for t in range(half_groups, KVH)]
 
     barrier = pltpu.get_barrier_semaphore()
     for k in range(1, n_dp):
@@ -277,9 +277,24 @@
         lax.broadcasted_iota(jnp.int32, (lat, seq), 0) + slot
         == lax.broadcasted_iota(jnp.int32, (lat, seq), 1)
     )
-    taken = dot(jnp.where(take, 1.0, 0.0).astype(BF16), grads[0]).astype(BF16)
-
-    def upstream(t):
+    t_own[...] = dot(jnp.where(take, 1.0, 0.0).astype(BF16), grads[0]).astype(BF16)
+    pl.semaphore_wait(barrier, n_dp + n_mp - 2)
+    t_pair = pair_copy(t_own, t_recv, 0)
+    t_pair.start()
+
+    features_in.wait()
+    wide = features[0].astype(F32)
+    mean_square = jnp.mean(wide * wide, axis=-1, keepdims=True)
+    features[0] = (wide * lax.rsqrt(mean_square + epsilon) * gain[...]).astype(BF16)
+
+    wk_in.wait()
+    projected_keys = dot(features[0], wk[...])
+    keys_t[...] = projected_keys.T.astype(BF16)
+    for g in range(KVH):
+        keys[g] = projected_keys[:, g * HEAD : (g + 1) * HEAD].astype(BF16)
+    t_pair.wait()
+    taken = t_own[...] + t_recv[...]
+    for t in range(half_groups):
         wo_in[t].wait()
         up = lax.dot_general(
             taken,
@@ -287,31 +302,9 @@
             (((1,), (1,)), ((), ())),
             preferred_element_type=F32,
         )
-        owner = 1 - core if t < half_groups else core
-        u_own[owner, pl.ds((t % half_groups) * HEAD, HEAD), :] = to_cols(up).astype(BF16)
-
-    for t in range(half_groups):
-        upstream(t)
-    pl.semaphore_wait(barrier, n_dp + n_mp - 2)
-    u_pair = pair_copy(u_own.at[1 - core], u_recv, 0)
-    u_pair.start()
-    for t in range(half_groups, KVH):
-        upstream(t)
+        u_all[chip, core, pl.ds(t * HEAD, HEAD), :] = to_cols(up).astype(BF16)
     u_gather = Gather(chips, chip, core, lambda j, c: u_all.at[j, c], u_send, u_got)
-    u_pair.wait()
-    u_all[chip, core] = u_own[core] + u_recv[...]
     u_gather.start()
-
-    features_in.wait()
-    wide = features[0].astype(F32)
-    mean_square = jnp.mean(wide * wide, axis=-1, keepdims=True)
-    features[0] = (wide * lax.rsqrt(mean_square + epsilon) * gain[...]).astype(BF16)
-
-    wk_in.wait()
-    projected_keys = dot(features[0], wk[...])
-    keys_t[...] = projected_keys.T.astype(BF16)
-    for g in range(KVH):
-        keys[g] = projected_keys[:, g * HEAD : (g + 1) * HEAD].astype(BF16)
     wv_in.wait()
     projected_values = dot(features[0], wv[...])
     values_t[...] = projected_values.T.astype(BF16)
@@ -541,6 +534,8 @@
     row_at = lax.broadcasted_iota(jnp.int32, (seq, 1), 0)
     inside = (row_at >= slot) & (row_at < slot + lat)
     text_in.wait()
+    for t in range(half_groups, KVH):
+        wo_in[t].wait()
     projected = dot(shifted, wo[...]).astype(BF16)
     merged[0] = jnp.where(inside, projected.astype(F32), text[0].astype(F32)).astype(BF16)
 
@@ -593,8 +588,8 @@
             pltpu.VMEM((KVH, tok, cols), F32),
             pltpu.VMEM((KVH, tok, cols), F32),
             pltpu.VMEM((2, KVH, HEAD, cols), F32),
-            pltpu.VMEM((2, half, cols), BF16),
-            pltpu.VMEM((half, cols), BF16),
+            pltpu.VMEM((lat, dm), BF16),
+            pltpu.VMEM((lat, dm), BF16),
             pltpu.VMEM((chips, 2, half, cols), BF16),
             pltpu.VMEM((chips, 2, 4 * KVH, cols), F32),
             pltpu.VMEM((chips, 2, 2 * KVH, cols), F32),

time: 38.2 us -> 38.5 us (level)
  Pallas kernels: 35.8 us -> 36.2 us
where the time goes in v3:
time: 38.5 us; the launch traced here: 38.3 us
  Pallas kernels  36.2 us (94%)
  local copies, waits for them, and re-layouts  1.54 us (4%)
  between operations  0.64 us (2%)
    pallas_call x1, Pallas kernels, on_device(): pl.pallas_call(functools.partial(kernel, (n_dp, n_mp, images, lat, tok, s...  36.2 us
    unnamed x2, local copies, waits for them, and re-layouts  1.54 us

profile of v3, /device:TPU:0, one launch (start us, length us, event | category | flops | bytes accessed | tf_op | source)
XLA Modules:
  0.0 38.3 jit_solution(3163566834771987435)
XLA Ops:
  0.6 36.2 %resampler.1 = (bf16[1,128,2048]{2,1,0:T(8,128)(2,1)S(1)}, f32[64,1536]{1,0:T(8,128)S(1)}) custom-call(s32[1,2]{1,0:T(1,128)} %tiles.1, s32[1,2]{1,0:T(1,128)} %slots.1, f32[1152]{0:T(1024)} %gain.1, bf16[64,1536]{1,0:T(8,128)(2,1)} %queries.1, bf16[1,512,1152]{2,1,0:T(8,128)(2,1)} %features_hbm.1, bf16[1152,384]{1,0:T(8,128)(2,1)} %wk_hbm.1, ...), custom_call_target="tpu_custom_call" | custom-call | tf_op jit(solution)/shard_map/resampler/pallas_call | solution.py:568
  36.8 0.8 %copy.14 = bf16[1,128,2048]{2,1,0:T(8,128)(2,1)} copy(bf16[1,128,2048]{2,1,0:T(8,128)(2,1)S(1)} %get-tuple-element.2) | data formatting | bytes 1048576
  37.6 0.7 %copy.15 = f32[64,1536]{1,0:T(8,128)} copy(f32[64,1536]{1,0:T(8,128)S(1)} %get-tuple-element.3) | data formatting | bytes 786432
